TPU v7x, 256 devices: a whole 4x4x8 slice. The times are simulated.
256 devices in a mesh: rep: 32 (over y, z_hi, core), dom: 8 (over z_lo, x).
Axes of the slice: x: 4, y: 4, z: 8 (z_hi: 4, z_lo: 2; z = z_hi * 2 + z_lo), core: 2. Of those that a mesh axis runs over, the one named last changes fastest.
Arguments:
- atomic_locations: float32 [3, 32, 65536], P(None, 'rep', 'dom'), may hold values from -9 to 9
- atomic_speeds: float32 [3, 32, 65536], P(None, 'rep', 'dom'), may hold values from -6 to 6
- atomic_properties: float32 [3, 65536], P(None, 'dom'), as said below
- resident_tile_members: int32 [2, 32, 512], P(None, 'rep', 'dom'), may hold values from 0 to 63
- resident_tile_tally: int32 [32, 8], P('rep', 'dom'), may hold values from 1 to 64, as said below
- top_edge_groups: int32 [32, 256], P('rep', 'dom'), may hold values from 0 to 63, as said below
- bottom_edge_groups: int32 [32, 256], P('rep', 'dom'), may hold values from 0 to 63, as said below
- boundary_tile_slots: int32 [2, 32, 256], P(None, 'rep', 'dom'), may hold values from 0 to 31
- boundary_tile_tally: int32 [32, 8], P('rep', 'dom'), may hold values from 1 to 32, as said below
- spring_links: int32 [2, 32768], P(None, 'dom'), may hold values from 0 to 8191
- thermal_levels: float32 [32], replicated, may hold values from 1 to 4
- exchange_mate: int32 [32], replicated, may hold values from 0 to 31, as said below
Outputs:
- positions_out: float32 [3, 32, 65536], P(None, 'rep', 'dom')
- velocities_out: float32 [3, 32, 65536], P(None, 'rep', 'dom')
Inputs may be any that keep to these rules, and one draw needn't show every extreme that they name: `resident_tile_tally`: the slots of one domain beyond its live count are padding. `boundary_tile_tally`: the slots of one domain beyond its live count are padding. `top_edge_groups`: the 32 entries of one domain are distinct clusters of that domain. `bottom_edge_groups`: the 32 entries of one domain are distinct clusters of that domain. exchange_mate[r] is r, r - 1 or r + 1, and exchange_mate[exchange_mate[r]] = r; the slot pairs 0, 1 and 30, 31 always swap. `atomic_properties`: row 0 charges, row 1 strengths between 0.5 and 1.5, row 2 inverse masses between 0.5 and 2.
All inputs are finite; a program needn't handle non-finite values.
Results may differ from a plain program's by a relative error of at most 0.0003.
Values sent between devices are 32-bit elements; how exact they have to be, the bound alone decides.
No kernel may reach another device: no remote copies, remote signals or barrier semaphores. Data moves between devices by JAX's collectives and lax.ppermute only.
A program may use at most 64 MiB of HBM per device.

v0:
```python
import functools
import math

import jax
import jax.numpy as jnp
from jax import lax
from jax.experimental import pallas as pl
from jax.experimental.pallas import tpu as pltpu
from jax.sharding import PartitionSpec as P

CA = 128
STEPS = 2
TIME_STEP = 0.05

F32 = jnp.float32
BF16 = jnp.bfloat16
LOG2E = 1.4426950408889634
ROWS = 8
ROUNDS = 1
PIECES = 16
LAG_SCALE = 3
LAG_SUM = 6
EDGE_SCALE = 3
EDGE_SUM = 6
BOND_PULL = 2
BOND_SPREAD = 4
VMEM_LIMIT = 20 << 20
PACK_LIMIT = 60 << 20
PACK_FLOPS = 2000

SMEM = pl.BlockSpec(memory_space=pltpu.SMEM)
VMEM = pl.BlockSpec(memory_space=pltpu.VMEM)


def swapped(shard, axis, start, ring=False):
    devices = lax.axis_size(axis)
    pairs = []
    for i in range(start, devices if ring else devices - 1, 2):
        other = (i + 1) % devices
        pairs += [(i, other), (other, i)]
    return lax.ppermute(shard, axis, pairs)


def side_lists(tops, bottoms):
    odd = lax.rem(lax.axis_index("dom"), 2) == 1

    def first(k):
        return jnp.where(odd, bottoms[0, k], tops[0, k])

    def second(k):
        return jnp.where(odd, tops[0, k], bottoms[0, k])

    return odd, first, second


def halves(a):
    high = a.astype(BF16).astype(F32)
    return high, (a - high).astype(BF16).astype(F32)


def tile(cluster):
    return pl.ds(pl.multiple_of(cluster * ROWS, ROWS), ROWS)


def stack_rows(stack, base, rows):
    for k, row in enumerate(rows):
        count = rows[0].shape[0]
        if not hasattr(row, "shape"):
            row = jnp.full((count, CA), row, F32)
        stack[pl.ds(base * ROWS + k, count, stride=ROWS), :] = row


def position_parts(x, y, z):
    (xh, xm), (yh, ym), (zh, zm) = halves(x), halves(y), halves(z)
    x, y, z = xh + xm, yh + ym, zh + zm
    norm = x * x + y * y + z * z + 0.25
    nh, nm = halves(norm)
    return (xh, yh, zh), (xm, ym, zm), (nh, nm, norm - nh - nm)


def near_stack(stacks, base, high, middle, norm):
    stack_rows(stacks.at[0], base, [*high, norm[0], 1.0, 1.0, norm[2], 0.0])
    stack_rows(stacks.at[1], base, [*middle, norm[1], 0.0, 0.0, 0.0, 0.0])


def far_stack(stacks, high, middle, norm):
    twice = [-2.0 * a for a in high]
    stack_rows(stacks.at[2], 0, [*twice, 1.0, norm[0], norm[2], 1.0, 0.0])
    stack_rows(stacks.at[3], 0, [*[-2.0 * a for a in middle], 0.0, norm[1], 0.0, 0.0, 0.0])


def fill_ratio(ratio, rho, base):
    for c in range(rho.shape[0]):
        ratio[base + c] = jnp.transpose(jnp.broadcast_to(rho[c : c + 1], (CA, CA)))


def moment_stack(stack, base, x, y, z, strength):
    g = strength * math.exp(0.25)
    parts = [halves(a) for a in (g * x, g * y, g * z, g)]
    stack_rows(stack, base, [p[0] for p in parts] + [p[1] for p in parts])


def both_orders(stacks, k, c):
    h, m = stacks[k, tile(c), :], stacks[k + 1, tile(c), :]
    return (
        jnp.concatenate([h, m], axis=0).astype(BF16),
        jnp.concatenate([m, h], axis=0).astype(BF16),
    )


def fill_near(near, stacks, c):
    near[c] = both_orders(stacks, 0, c)[0]


def fill_far(far, stacks, c):
    far[c, 0], far[c, 1] = both_orders(stacks, 2, c)


def fill_moments(moments, stack, c):
    w = stack[tile(c), :]
    moments[c] = jnp.concatenate([w, jnp.zeros_like(w)], axis=0).astype(BF16)


def distances(near, far, pair, other):
    left = [near[i] for i, _ in (pair, other)]
    left = jnp.transpose(jnp.concatenate([left[0], left[0], left[1], left[1]], axis=0))
    right = [jnp.concatenate([far[j, 0], far[j, 1]], axis=0) for _, j in (pair, other)]
    zero = jnp.zeros_like(right[0])
    right = jnp.concatenate(
        [
            jnp.concatenate([right[0], zero], axis=1),
            jnp.concatenate([zero, right[1]], axis=1),
        ],
        axis=0,
    )
    both = jnp.dot(left, right, preferred_element_type=F32)
    return both[:, :CA], both[:, CA:]


def charge_ratio(charge, strength):
    return charge / strength * math.exp(-0.125)


def pair_scale(t, near_rho, far_rho):
    r = lax.rsqrt(t)
    c = jnp.exp2(t * (-0.5 * LOG2E)) + (near_rho * far_rho) * (r * r * r)
    high = c.astype(BF16)
    return high, (c - high.astype(F32)).astype(BF16)


def moment_sums(weights, scales):
    sums = jnp.dot(weights, scales, preferred_element_type=F32)[:ROWS]
    return sums[:, :CA] + sums[:, CA:]


def split(a, parts):
    return halves(a) if parts == 2 else (a,)


def bond_table(x, parts):
    half = x.shape[1] // 2

    def lay(v):
        flat = (3 * half, CA)
        return jnp.concatenate([v[:, :half].reshape(flat), v[:, half:].reshape(flat)], axis=1)

    return jnp.concatenate([lay(part) for part in split(x, parts)], axis=0).astype(BF16)


def bond_picks(picks, masks, atoms, start):
    size = atoms.shape[1]
    half = masks.shape[1]
    lane_id = lax.broadcasted_iota(jnp.int32, (2 * CA, size), 0).astype(F32).astype(BF16)
    row_id = lax.broadcasted_iota(jnp.int32, (half, size), 0)
    one, none = jnp.ones((), BF16), jnp.zeros((), BF16)
    for e in range(2):
        atom = atoms[e : e + 1]
        cluster = atom // CA
        lane = (atom % CA + cluster // half * CA).astype(F32).astype(BF16)
        hit = lane_id == jnp.broadcast_to(lane, lane_id.shape)
        picks[e, :, pl.ds(start, size)] = jnp.where(hit, one, none)
        mask = jnp.where(row_id == cluster % half, 1.0, 0.0)
        masks[e, :, pl.ds(start, size)] = mask.astype(BF16)


def bond_gather(table, picks, start, size):
    return [
        jnp.dot(table, picks[e, :, pl.ds(start, size)], preferred_element_type=F32)
        for e in range(2)
    ]


def bond_pull(rows, masks, start, size):
    half = masks.shape[1]
    parts = rows[0].shape[0] // (3 * half)
    ends = []
    for e in range(2):
        mask = masks[e, :, pl.ds(start, size)].astype(F32)
        both = sum(rows[e][k * 3 * half : (k + 1) * 3 * half] for k in range(parts))
        ends.append(jnp.sum(both.reshape(3, half, size) * mask[None], axis=1))
    return split(ends[1] - ends[0], parts)


def bond_scatter(pull, picks, masks, start, size):
    half = masks.shape[1]
    total = None
    for e, sign in enumerate((1.0, -1.0)):
        mask = masks[e, :, pl.ds(start, size)]
        spread = [
            mask * jnp.broadcast_to(sign * part[c : c + 1], (half, size)).astype(BF16)
            for part in pull
            for c in range(3)
        ]
        term = lax.dot_general(
            jnp.concatenate(spread, axis=0),
            picks[e, :, pl.ds(start, size)],
            (((1,), (1,)), ((), ())),
            preferred_element_type=F32,
        )
        total = term if total is None else total + term
    return total


def pair_moments(moments, i, j, scale):
    high, low = scale
    on_far = moment_sums(moments[i], jnp.concatenate([high, low], axis=1))
    turned = jnp.concatenate([jnp.transpose(high), jnp.transpose(low)], axis=1)
    return moment_sums(moments[j], turned), on_far


def local_kernel(first, pairs, tally, x_ref, props, *rest):
    if first:
        raw = props
        bonds, acc, bonded, far, rho, props, picks, masks, ratio, *scratch = rest
        relay_properties(raw, props)
    else:
        x_before, bonded_before, picks, masks, ratio, acc, bonded, far, rho, *scratch = rest
    stacks, moment_rows, near, moments, table, bond_sums = scratch
    clusters = x_ref.shape[1]
    half = clusters // 2
    group = pairs.shape[1] // ROUNDS
    size = picks.shape[2] // ROUNDS
    x, y, z = x_ref[0], x_ref[1], x_ref[2]
    parts = position_parts(x, y, z)
    rho[...] = charge_ratio(props[0], props[1])
    if first:
        fill_ratio(ratio, rho[...], 0)
    near_stack(stacks, 0, *parts)
    far_stack(stacks, *parts)
    moment_stack(moment_rows, 0, x, y, z, props[1])
    for c in range(clusters):
        fill_near(near, stacks, c)
        fill_far(far, stacks, c)
        fill_moments(moments, moment_rows, c)
    acc[...] = jnp.zeros_like(acc)
    if first:
        table[...] = bond_table(x_ref[...], 2)
    else:
        table[...] = bond_table(x_ref[...] - x_before[...], 1)
    bond_sums[...] = jnp.zeros_like(bond_sums)
    live = jnp.broadcast_to(tally[...], (ROWS, CA))

    def round_of(block, carry):
        start = pl.multiple_of(block * size, size)
        if first:
            bond_picks(picks, masks, bonds[:, pl.ds(start, size)], start)
        slots = [block * group + k for k in range(group)]
        ends = [(pairs[0, s], pairs[1, s]) for s in slots]
        piece = size // PIECES
        steps = group // PIECES
        products, scales, sums = [None] * group, [None] * group, [None] * group
        gathered, pulls, spread = [None] * PIECES, [None] * PIECES, None
        for t in range(group + LAG_SUM):
            if t < group and t % 2 == 0:
                products[t : t + 2] = distances(near, far, ends[t], ends[t + 1])
            q = t // steps
            if t % steps == 0 and q < PIECES:
                gathered[q] = bond_gather(table[...], picks, start + q * piece, piece)
            q = (t - BOND_PULL) // steps
            if (t - BOND_PULL) % steps == 0 and 0 <= q < PIECES:
                pulls[q] = bond_pull(gathered[q], masks, start + q * piece, piece)
            q = t - LAG_SCALE
            if 0 <= q < group:
                i, j = ends[q]
                scales[q] = pair_scale(products[q], ratio[i], rho[pl.ds(j, 1), :])
            q = t - LAG_SUM
            if 0 <= q < group:
                sums[q] = pair_moments(moments, *ends[q], scales[q])
            q = (t - BOND_SPREAD) // steps
            if (t - BOND_SPREAD) % steps == 0 and 0 <= q < PIECES:
                part = bond_scatter(pulls[q], picks, masks, start + q * piece, piece)
                spread = part if spread is None else spread + part
        bond_sums[...] += spread
        for s, (i, j), (on_near, on_far) in zip(slots, ends, sums):
            weight = jnp.where(live > s, jnp.where(i == j, 0.5, 1.0), 0.0)
            acc[tile(i), :] += weight * on_near
            acc[tile(j), :] += weight * on_far
        return carry

    lax.fori_loop(0, ROUNDS, round_of, 0)
    for c in range(3):
        both = bond_sums[pl.ds(c * half, half), :]
        if first:
            both = both + bond_sums[pl.ds((3 + c) * half, half), :]
        for k in range(2):
            new = both[:, k * CA : (k + 1) * CA]
            if not first:
                new = new + bonded_before[c, pl.ds(k * half, half), :]
            bonded[c, pl.ds(k * half, half), :] = new


def edge_kernel(first, last, kick, tops, bottoms, slots, *rest):
    if last:
        levels, mates, *rest = rest
    tally, x_ref, v_ref, props, acc_in, bonded, far, rho, *rest = rest
    first_x, second_x, first_start, second_start, *rest = rest
    *rest, stacks, moment_rows, near, moments, acc, indices, lower, arrived = rest
    if last:
        ratio, state, choice = rest
        exchange_choice(levels, mates, choice)
    elif first:
        x_out, v_out, to_first, to_second, ratio = rest
    else:
        ratio, x_out, v_out, to_first, to_second = rest
    odd, _, _ = side_lists(tops, bottoms)
    rows = [start[5, pl.ds(0, ROWS), :] for start in (first_start, second_start)]
    indices[...] = jnp.where(odd, rows[0], rows[1]).astype(jnp.int32)
    indices[pl.ds(3, 1), pl.ds(0, 1)] = tally[...]
    fetch = pltpu.make_async_copy(indices, lower, arrived)
    fetch.start()
    clusters = x_ref.shape[1]
    facing = first_x.shape[1]
    for side, (hx, hp) in enumerate(((first_x, first_start), (second_x, second_start))):
        if first:
            fill_ratio(ratio, charge_ratio(hp[3], hp[4]), side * facing)
        near_stack(stacks, side * facing, *position_parts(hx[0], hx[1], hx[2]))
        moment_stack(moment_rows, side * facing, hx[0], hx[1], hx[2], hp[4])
    for c in range(2 * facing):
        fill_near(near, stacks, c)
        fill_moments(moments, moment_rows, c)
    acc[...] = acc_in[...]

    width = slots.shape[1]
    upper_base = jnp.where(odd, facing, 0)
    lower_base = facing - upper_base
    fetch.wait()
    ends, weights = [], []
    for s in range(width):
        ends.append((upper_base + slots[1, s], tops[0, slots[0, s]]))
        weights.append(jnp.where(s < lower[3, 0], 1.0, 0.0))
        ends.append((lower_base + lower[0, s], bottoms[0, lower[1, s]]))
        weights.append(jnp.where(s < lower[2, 0], 1.0, 0.0))
    count = len(ends)
    products, scales = [None] * count, [None] * count
    for t in range(count + EDGE_SUM):
        if t < count and t % 2 == 0:
            products[t : t + 2] = distances(near, far, ends[t], ends[t + 1])
        q = t - EDGE_SCALE
        if 0 <= q < count:
            j, i = ends[q]
            scales[q] = pair_scale(products[q], ratio[j], rho[pl.ds(i, 1), :])
        q = t - EDGE_SUM
        if 0 <= q < count:
            j, i = ends[q]
            total = moment_sums(moments[j], jnp.concatenate(scales[q], axis=1))
            acc[tile(i), :] += weights[q] * total

    def moment(k):
        high = acc[pl.ds(k, clusters, stride=ROWS), :]
        return high + acc[pl.ds(k + 4, clusters, stride=ROWS), :]

    mass = kick * props[2]
    g = props[1]
    count = moment(3)
    for c in range(3):
        force = g * (x_ref[c] * count - moment(c)) + bonded[c]
        v = v_ref[c] + mass * force
        if last:
            state[c] = x_ref[c]
            state[3 + c] = v
        else:
            v_out[c] = v
            x_out[c] = x_ref[c] + TIME_STEP * v
    if not last:
        pack_rows(tops, bottoms, x_out, to_first, to_second, 0, 3)


def pack_rows(tops, bottoms, source, to_first, to_second, base, count):
    _, first, second = side_lists(tops, bottoms)
    for k in range(to_first.shape[1]):
        i, j = first(k), second(k)
        rows = [[source[c, pl.ds(n, 1), :] for c in range(count)] for n in (i, j)]
        for c in range(count):
            to_first[base + c, pl.ds(k, 1), :] = rows[0][c]
            to_second[base + c, pl.ds(k, 1), :] = rows[1][c]


def relay_properties(raw, props):
    for c in range(props.shape[0]):
        for k in range(props.shape[1]):
            props[c, pl.ds(k, 1), :] = raw[pl.ds(c, 1), pl.ds(k * CA, CA)]


def pack_kernel(tops, bottoms, x_ref, raw, slots, tally, to_first, to_second, props):
    relay_properties(raw, props)
    width = slots.shape[1]
    for buffer in (to_first, to_second):
        buffer[5] = jnp.zeros(buffer.shape[1:], F32)
        buffer[5, pl.ds(0, 2), pl.ds(0, width)] = slots[...].astype(F32)
        buffer[5, pl.ds(2, 1), pl.ds(0, 1)] = tally[...].astype(F32)
    pack_rows(tops, bottoms, x_ref, to_first, to_second, 0, 3)
    pack_rows(tops, bottoms, props, to_first, to_second, 3, 2)


def exchange_choice(levels, mates, choice):
    own = lax.axis_index("rep")
    mate = mates[own]
    near_mate = own + 1 - 2 * lax.rem(own, 2)
    row = (1, CA)
    ratio = jnp.full(row, levels[own], F32) / jnp.full(row, levels[mate], F32)
    choice[...] = jnp.zeros_like(choice)
    choice[pl.ds(0, 1), :] = jnp.full(row, jnp.where(mate == own, 1.0, 0.0), F32)
    choice[pl.ds(1, 1), :] = jnp.full(row, jnp.where(mate == near_mate, 1.0, 0.0), F32)
    choice[pl.ds(2, 1), :] = jnp.sqrt(ratio)


def local(
    atomic_locations,
    atomic_speeds,
    atomic_properties,
    resident_tile_members,
    resident_tile_tally,
    top_edge_groups,
    bottom_edge_groups,
    boundary_tile_slots,
    boundary_tile_tally,
    spring_links,
    thermal_levels,
    exchange_mate,
):
    atoms = atomic_locations.shape[2]
    clusters = atoms // CA
    facing = top_edge_groups.shape[1]
    shape = (3, clusters, CA)
    x = atomic_locations.reshape(shape)
    v = atomic_speeds.reshape(shape)
    pairs = resident_tile_members[:, 0]
    slots = boundary_tile_slots[:, 0]
    sds = jax.ShapeDtypeStruct
    params = pltpu.CompilerParams(vmem_limit_bytes=VMEM_LIMIT)

    to_first, to_second = pl.pallas_call(
        pack_kernel,
        out_shape=(sds((6, facing, CA), F32),) * 2,
        in_specs=[SMEM] * 2 + [VMEM] * 4,
        out_specs=(VMEM,) * 2,
        scratch_shapes=[pltpu.VMEM((2,) + shape[1:], F32)],
        compiler_params=pltpu.CompilerParams(vmem_limit_bytes=PACK_LIMIT),
        cost_estimate=pl.CostEstimate(
            flops=PACK_FLOPS * 1_000_000, bytes_accessed=1_000_000, transcendentals=0
        ),
        name="pack",
    )(
        top_edge_groups,
        bottom_edge_groups,
        x,
        atomic_properties,
        slots,
        boundary_tile_tally,
    )
    first_start = swapped(to_first, "dom", 0, True)
    second_start = swapped(to_second, "dom", 1, True)

    def scratch(sources):
        return [
            pltpu.VMEM((4, clusters * ROWS, CA), F32),
            pltpu.VMEM((clusters * ROWS, CA), F32),
            pltpu.VMEM((sources, 2 * ROWS, CA), BF16),
            pltpu.VMEM((sources, 2 * ROWS, CA), BF16),
        ]

    bonds = spring_links.shape[1]
    kept = (
        sds(shape, F32),
        sds((2, 2 * CA, bonds), BF16),
        sds((2, clusters // 2, bonds), BF16),
        sds((clusters, CA, CA), F32),
    )

    def local_call(first):
        sums = (
            sds((clusters * ROWS, CA), F32),
            sds(shape, F32),
            sds((clusters, 2, 2 * ROWS, CA), BF16),
            sds((clusters, CA), F32),
        )
        rows = 3 * clusters if first else 3 * clusters // 2
        return pl.pallas_call(
            functools.partial(local_kernel, first),
            out_shape=sums + kept if first else sums,
            in_specs=[SMEM] + [VMEM] * (4 if first else 8),
            out_specs=(VMEM,) * (8 if first else 4),
            scratch_shapes=scratch(clusters)
            + [
                pltpu.VMEM((rows, 2 * CA), BF16),
                pltpu.VMEM((rows, 2 * CA), F32),
            ],
            compiler_params=params,
            cost_estimate=pl.CostEstimate(
                flops=2_000_000_000, bytes_accessed=1_000_000, transcendentals=2_000_000
            ),
            name="resident",
        )

    def edge_call(first, last, kick):
        if last:
            outs = (sds((6, clusters, CA), F32), sds((ROWS, CA), F32))
        else:
            outs = (sds(shape, F32),) * 2 + (sds((3, facing, CA), F32),) * 2
        if first:
            outs += (sds((2 * facing, CA, CA), F32),)
        return pl.pallas_call(
            functools.partial(edge_kernel, first, last, kick),
            out_shape=outs,
            in_specs=[SMEM] * (5 if last else 3) + [VMEM] * (12 if first else 13),
            out_specs=(VMEM,) * len(outs),
            scratch_shapes=scratch(2 * facing)
            + [
                pltpu.VMEM((clusters * ROWS, CA), F32),
                pltpu.VMEM((ROWS, CA), jnp.int32),
                pltpu.SMEM((ROWS, CA), jnp.int32),
                pltpu.SemaphoreType.DMA,
            ],
            compiler_params=params,
            cost_estimate=pl.CostEstimate(
                flops=1_000_000_000, bytes_accessed=1_000_000, transcendentals=2_000_000
            ),
            name="edges",
        )

    halo_ratio = ()
    first_x, second_x = first_start, second_start
    for step in range(STEPS + 1):
        if step == 0:
            acc, bonded, far, rho, props, *static = local_call(True)(
                pairs, resident_tile_tally, x, atomic_properties, spring_links
            )
        else:
            acc, bonded, far, rho = local_call(False)(
                pairs, resident_tile_tally, x, props, x_before, bonded, *static
            )
        last = step == STEPS
        kick = TIME_STEP * (0.5 if step == 0 or last else 1.0)
        results = edge_call(step == 0, last, kick)(
            top_edge_groups,
            bottom_edge_groups,
            slots,
            *((thermal_levels, exchange_mate) if last else ()),
            boundary_tile_tally,
            x,
            v,
            props,
            acc,
            bonded,
            far,
            rho,
            first_x,
            second_x,
            first_start,
            second_start,
            *halo_ratio,
        )
        if last:
            state, choice = results
        else:
            x_before = x
            x, v, to_first, to_second, *new_ratio = results
            halo_ratio = halo_ratio or new_ratio
            first_x = swapped(to_first, "dom", 0, True)
            second_x = swapped(to_second, "dom", 1, True)

    keep, near_mate, ratio = choice[0] > 0.5, choice[1] > 0.5, choice[2]
    slot = jnp.arange(exchange_mate.shape[0], dtype=jnp.int32)
    crossing = jnp.any((exchange_mate != slot) & (exchange_mate != (slot ^ 1)))

    def exchanged(state, *others):
        def part(k):
            own, *rest = [a[3 * k : 3 * k + 3] for a in (state, *others)]
            other = jnp.where(near_mate, *rest) if len(rest) == 2 else rest[0]
            return jnp.where(keep, own, other)

        return part(0), part(1) * ratio

    def with_crossing(state):
        return exchanged(state, swapped(state, "rep", 0), swapped(state, "rep", 1))

    def without_crossing(state):
        return exchanged(state, swapped(state, "rep", 0))

    new_x, new_v = lax.cond(crossing, with_crossing, without_crossing, state)
    return new_x.reshape(3, 1, atoms), new_v.reshape(3, 1, atoms)


def solution(mesh):
    placed = (
        P(None, "rep", "dom"),
        P(None, "rep", "dom"),
        P(None, "dom"),
        P(None, "rep", "dom"),
        P("rep", "dom"),
        P("rep", "dom"),
        P("rep", "dom"),
        P(None, "rep", "dom"),
        P("rep", "dom"),
        P(None, "dom"),
        P(),
        P(),
    )
    return jax.shard_map(
        local,
        mesh=mesh,
        in_specs=placed,
        out_specs=(P(None, "rep", "dom"), P(None, "rep", "dom")),
        check_vma=False,
    )
```

profile of v0, /device:TPU:1, one launch (start us, length us, event | category | flops | bytes accessed | tf_op | source)
XLA Modules:
  0.0 45.9 jit_solution(14686369852620661830)
XLA Ops:
  0.6 0.0 copy-start
  0.6 0.0 copy-start.7
  0.7 0.0 copy-start.5
  1.4 1.9 %pack.1 = (f32[6,32,128]{2,1,0:T(8,128)}, f32[6,32,128]{2,1,0:T(8,128)}) custom-call(s32[1,32]{1,0:T(1,128)} %tops.7, s32[1,32]{1,0:T(1,128)} %bottoms.7, f32[3,64,128]{2,1,0:T(8,128)} %bitcast.11, f32[3,8192]{1,0:T(4,128)} %raw.1, s32[2,32]{1,0:T(2,128)} %bitcast.18, s32[1,1]{1,0:T(1,128)S(6)} %copy.23.tally.rest_0_.rest_2_), custom_call_target="tpu_custom_call" | custom-call | flops 2000000000 | bytes 1000000 | tf_op jit(solution)/shard_map/pack/pallas_call | solution.py:452
  3.3 0.0 copy-start.8
  3.3 2.1 %collective-permute-start.3 = (f32[6,32,128]{2,1,0:T(8,128)}, f32[6,32,128]{2,1,0:T(8,128)S(1)}, u32[]{:S(2)}, u32[]{:S(2)}) collective-permute-start(f32[6,32,128]{2,1,0:T(8,128)} %get-tuple-element.74), channel_id=1, source_target_pairs={{0,1},{1,0},{2,3},{3,2},{4,5},{5,4},{6,7},{7,6},{8,9},{9,8},{10,11... | collective-permute-start | bytes 294920 | tf_op jit(solution)/shard_map/ppermute | solution.py:41
  5.4 3.2 %collective-permute-start.4 = (f32[6,32,128]{2,1,0:T(8,128)}, f32[6,32,128]{2,1,0:T(8,128)S(1)}, u32[]{:S(2)}, u32[]{:S(2)}) collective-permute-start(f32[6,32,128]{2,1,0:T(8,128)} %get-tuple-element.75), channel_id=1, source_target_pairs={{1,2},{2,1},{3,4},{4,3},{5,6},{6,5},{7,0},{0,7},{9,10},{10,9},{11,... | collective-permute-start | bytes 294920 | tf_op jit(solution)/shard_map/ppermute | solution.py:41
  9.2 0.7 %and_reduce_fusion = pred[]{:T(512)} fusion(s32[32]{0:T(128)S(1)} %copy-done.5), kind=kLoop, calls=%fused_computation.6 | loop fusion | flops 159 | bytes 129 | tf_op jit(solution)/shard_map/reduce_or | solution.py:584
  10.5 0.0 copy-done
  10.5 0.0 copy-done.7
  10.6 0.0 copy-done.1
  10.6 0.0 copy-done.9
  10.6 6.4 %resident.3 = (f32[512,128]{1,0:T(8,128)S(1)}, f32[3,64,128]{2,1,0:T(8,128)S(1)}, bf16[64,2,16,128]{3,2,1,0:T(8,128)(2,1)S(1)}, f32[64,128]{1,0:T(8,128)S(1)}, f...) custom-call(s32[2,64]{1,0:T(2,128)S(1)} %bitcast.15, ...), custom_call_target="tpu_custom_call" | custom-call | flops 2000000000 | bytes 1000000 | tf_op jit(solution)/shard_map/resident/pallas_call | solution.py:545
  17.0 0.0 collective-permute-done.3.rest_8_.rest_10_.rest_12_
  17.0 0.0 collective-permute-done.4.rest_9_.rest_11_.rest_13_
  17.1 4.4 %edges.3 = (f32[3,64,128]{2,1,0:T(8,128)S(1)}, f32[3,64,128]{2,1,0:T(8,128)S(1)}, f32[3,32,128]{2,1,0:T(8,128)S(1)}, f32[3,32,128]{2,1,0:T(8,128)S(1)}, f32[64,128,128]{2,1,0:T(8,128)S(1)}) custom-call(s32[1,32]{1,0:T(1,128)S(1)} %copy-done.3, s32[1,32]{1,0:T(1,128)S(1)} %copy-done.4, s32[2,32]{1,0:T(2,128)S(1)} %bitcast.19, ...), custom_call_target="tpu_custom_call" | custom-call | flops 1000000000 | bytes 1000000 | tf_op jit(solution)/shard_map/edges/pallas_call | solution.py:554
  21.5 0.1 collective-permute-start.5
  21.6 0.9 %collective-permute-start.6 = (f32[3,32,128]{2,1,0:T(8,128)S(1)}, f32[3,32,128]{2,1,0:T(8,128)S(1)}, u32[]{:S(2)}, u32[]{:S(2)}) collective-permute-start(f32[3,32,128]{2,1,0:T(8,128)S(1)} %get-tuple-element.86), channel_id=1, source_target_pairs={{1,2},{2,1},{3,4},{4,3},{5,6},{6,5},{7,0},{0,7},{9,10},{10,9},{11,... | collective-permute-start | bytes 147464 | tf_op jit(solution)/shard_map/ppermute | solution.py:41
  22.5 4.8 %resident.4 = (f32[512,128]{1,0:T(8,128)S(1)}, f32[3,64,128]{2,1,0:T(8,128)S(1)}, bf16[64,2,16,128]{3,2,1,0:T(8,128)(2,1)S(1)}, f32[64,128]{1,0:T(8,128)S(1)}) custom-call(s32[2,64]{1,0:T(2,128)S(1)} %bitcast.16, s32[1,1]{1,0:T(1,128)S(6)} %copy.22.tally, f32[3,64,128]{2,1,0:T(8,128)S(1)} %get-tuple-element.76.x_ref.rest_1_.rest_0_, ...), custom_call_target="tpu_custom_call" | custom-call | flops 2000000000 | bytes 1000000 | tf_op jit(solution)/shard_map/resident/pallas_call | solution.py:549
  27.3 0.0 collective-permute-done.5.rest_8_
  27.3 0.0 collective-permute-done.6.rest_9_
  27.3 3.4 %edges.4 = (f32[3,64,128]{2,1,0:T(8,128)S(1)}, f32[3,64,128]{2,1,0:T(8,128)S(1)}, f32[3,32,128]{2,1,0:T(8,128)S(1)}, f32[3,32,128]{2,1,0:T(8,128)S(1)}) custom-call(s32[1,32]{1,0:T(1,128)S(1)} %copy-done.3, s32[1,32]{1,0:T(1,128)S(1)} %copy-done.4, s32[2,32]{1,0:T(2,128)S(1)} %bitcast.20, s32[1,1]{1,0:T(1,128)S(6)} %copy.23.tally.rest_0_.rest_2_, ...), custom_call_target="tpu_custom_call" | custom-call | flops 1000000000 | bytes 1000000 | tf_op jit(solution)/shard_map/edges/pallas_call | solution.py:554
  30.7 0.9 %collective-permute-start.7 = (f32[3,32,128]{2,1,0:T(8,128)S(1)}, f32[3,32,128]{2,1,0:T(8,128)S(1)}, u32[]{:S(2)}, u32[]{:S(2)}) collective-permute-start(f32[3,32,128]{2,1,0:T(8,128)S(1)} %get-tuple-element.94), channel_id=1, source_target_pairs={{0,1},{1,0},{2,3},{3,2},{4,5},{5,4},{6,7},{7,6},{8,9},{9,8},{10,11... | collective-permute-start | bytes 147464 | tf_op jit(solution)/shard_map/ppermute | solution.py:41
  31.6 2.4 %collective-permute-start.8 = (f32[3,32,128]{2,1,0:T(8,128)S(1)}, f32[3,32,128]{2,1,0:T(8,128)S(1)}, u32[]{:S(2)}, u32[]{:S(2)}) collective-permute-start(f32[3,32,128]{2,1,0:T(8,128)S(1)} %get-tuple-element.95), channel_id=1, source_target_pairs={{1,2},{2,1},{3,4},{4,3},{5,6},{6,5},{7,0},{0,7},{9,10},{10,9},{11,... | collective-permute-start | bytes 147464 | tf_op jit(solution)/shard_map/ppermute | solution.py:41
  34.1 4.8 %resident.5 = (f32[512,128]{1,0:T(8,128)S(1)}, f32[3,64,128]{2,1,0:T(8,128)S(1)}, bf16[64,2,16,128]{3,2,1,0:T(8,128)(2,1)S(1)}, f32[64,128]{1,0:T(8,128)S(1)}) custom-call(s32[2,64]{1,0:T(2,128)S(1)} %bitcast.17, s32[1,1]{1,0:T(1,128)S(6)} %copy.22.tally, f32[3,64,128]{2,1,0:T(8,128)S(1)} %get-tuple-element.88.x_ref.rest_3_, ...), custom_call_target="tpu_custom_call" | custom-call | flops 2000000000 | bytes 1000000 | tf_op jit(solution)/shard_map/resident/pallas_call | solution.py:549
  38.8 0.0 collective-permute-done.7.rest_10_
  38.9 0.0 collective-permute-done.8.rest_11_
  38.9 3.3 %edges.5 = (f32[6,64,128]{2,1,0:T(8,128)S(1)}, f32[8,128]{1,0:T(8,128)S(1)}) custom-call(s32[1,32]{1,0:T(1,128)S(1)} %copy-done.3, s32[1,32]{1,0:T(1,128)S(1)} %copy-done.4, s32[2,32]{1,0:T(2,128)S(1)} %bitcast.21, f32[32]{0:T(128)S(1)} %copy-done.6, s32[32]{0:T(128)S(1)} %copy-done.5, s32[1,1]{1,0:T(1,128)S(6)} %copy.23.tally.rest_0_.rest_2_, ...), custom_call_target="tpu_custom_call" | custom-call | flops 1000000000 | bytes 1000000 | tf_op jit(solution)/shard_map/edges/pallas_call | solution.py:554
  42.2 3.0 %conditional.1 = (pred[3,64,128]{2,1,0:T(8,128)(4,1)S(1)}, pred[3,64,128]{2,1,0:T(8,128)(4,1)S(1)}, f32[3,64,128]{2,1,0:T(8,128)S(1)}, f32[6,64,128]{2,1,0:T(8,1...) conditional(s32[]{:T(128)} %convert_element_type.3, (pred[128]{0:T(512)(128)(4,1)S(1)}, ...), branch_computations={%region_1.2_spmd, %region_2.3_spmd} | conditional | flops 49280 | bytes 2212996 | solution.py:600
  42.2 1.9 %collective-permute-start.2 = (f32[6,64,128]{2,1,0:T(8,128)S(1)}, f32[6,64,128]{2,1,0:T(8,128)S(1)}, u32[]{:S(2)}, u32[]{:S(2)}) collective-permute-start(f32[6,64,128]{2,1,0:T(8,128)S(1)} %get-tuple-element.113), channel_id=1, source_target_pairs={{0,8},{8,0},{16,24},{24,16},{32,40},{40,32},{48,56},{56,48},{64,72... | collective-permute-start | bytes 589832 | tf_op jit(solution)/shard_map/cond/branch_0_fun/ppermute | solution.py:41
  44.1 1.1 %collective-permute-done.2 = f32[6,64,128]{2,1,0:T(8,128)S(1)} collective-permute-done((f32[6,64,128]{2,1,0:T(8,128)S(1)}, f32[6,64,128]{2,1,0:T(8,128)S(1)}, u32[]{:S(2)}, u32[]{:S(2)}) %collective-permute-start.2) | collective-permute-done | bytes 196640 | tf_op jit(solution)/shard_map/cond/branch_0_fun/ppermute | solution.py:41
  45.2 0.7 %select_multiply_fusion = (f32[3,64,128]{2,1,0:T(8,128)}, f32[3,64,128]{2,1,0:T(8,128)}) fusion(pred[3,64,128]{2,1,0:T(8,128)(4,1)S(1)} %get-tuple-element.98, f32[3,64,128]{2,1,0:T(8,128)S(1)} %get-tuple-element.101, f32[6,64,128]{2,1,0:T(8,128)S(1)} %get-tuple-element.99, f32[128]{0:T(128)S(1)} %bitcast.25, f32[3,64,128]{2,1,0:T(8,128)S(1)} %get-tuple-element.100), kind=kLoop, calls=%fused_computation.3 | loop fusion | flops 73728 | bytes 614912 | tf_op jit(solution)/shard_map/cond/branch_0_fun/mul | solution.py:592
  (17 shorter events, 0.1 us)
Async XLA Ops:
  0.6 9.9 %copy-start = (f32[3,1,8192]{2,1,0:T(1,128)S(1)}, f32[3,1,8192]{2,1,0:T(1,128)}, u32[]{:S(2)}) copy-start(f32[3,1,8192]{2,1,0:T(1,128)} %param.14) | copy-start | bytes 294916
  0.6 9.9 %copy-start.7 = (f32[3,8192]{1,0:T(4,128)S(1)}, f32[3,8192]{1,0:T(4,128)}, u32[]{:S(2)}) copy-start(f32[3,8192]{1,0:T(4,128)} %raw.1) | copy-start | bytes 294916
  0.7 8.6 %copy-start.5 = (s32[32]{0:T(128)S(1)}, s32[32]{0:T(128)}, u32[]{:S(2)}) copy-start(s32[32]{0:T(128)} %rest_1_.1) | copy-start | bytes 388
  0.7 9.9 %copy-start.1 = (s32[2,1,64]{2,1,0:T(1,128)S(1)}, s32[2,1,64]{2,1,0:T(1,128)}, u32[]{:S(2)}) copy-start(s32[2,1,64]{2,1,0:T(1,128)} %param.17) | copy-start | bytes 1540
  0.7 9.9 %copy-start.9 = (s32[2,4096]{1,0:T(2,128)S(1)}, s32[2,4096]{1,0:T(2,128)}, u32[]{:S(2)}) copy-start(s32[2,4096]{1,0:T(2,128)} %rest_0_.4) | copy-start | bytes 98308
  3.3 13.8 %copy-start.2 = (s32[2,1,32]{2,1,0:T(1,128)S(1)}, s32[2,1,32]{2,1,0:T(1,128)}, u32[]{:S(2)}) copy-start(s32[2,1,32]{2,1,0:T(1,128)} %param.21) | copy-start | bytes 772
  3.3 13.8 %copy-start.3 = (s32[1,32]{1,0:T(1,128)S(1)}, s32[1,32]{1,0:T(1,128)}, u32[]{:S(2)}) copy-start(s32[1,32]{1,0:T(1,128)} %tops.7) | copy-start | bytes 388
  3.3 13.8 %copy-start.4 = (s32[1,32]{1,0:T(1,128)S(1)}, s32[1,32]{1,0:T(1,128)}, u32[]{:S(2)}) copy-start(s32[1,32]{1,0:T(1,128)} %bottoms.7) | copy-start | bytes 388
  3.3 13.8 %copy-start.8 = (f32[3,1,8192]{2,1,0:T(1,128)S(1)}, f32[3,1,8192]{2,1,0:T(1,128)}, u32[]{:S(2)}) copy-start(f32[3,1,8192]{2,1,0:T(1,128)} %param.15) | copy-start | bytes 294916
  3.3 13.7 %collective-permute-start.3 = (f32[6,32,128]{2,1,0:T(8,128)}, f32[6,32,128]{2,1,0:T(8,128)S(1)}, u32[]{:S(2)}, u32[]{:S(2)}) collective-permute-start(f32[6,32,128]{2,1,0:T(8,128)} %get-tuple-element.74), channel_id=1, source_target_pairs={{0,1},{1,0},{2,3},{3,2},{4,5},{5,4},{6,7},{7,6},{8,9},{9,8},{10,11... | collective-permute-start | bytes 294920 | tf_op jit(solution)/shard_map/ppermute | solution.py:41
  5.4 11.6 %collective-permute-start.4 = (f32[6,32,128]{2,1,0:T(8,128)}, f32[6,32,128]{2,1,0:T(8,128)S(1)}, u32[]{:S(2)}, u32[]{:S(2)}) collective-permute-start(f32[6,32,128]{2,1,0:T(8,128)} %get-tuple-element.75), channel_id=1, source_target_pairs={{1,2},{2,1},{3,4},{4,3},{5,6},{6,5},{7,0},{0,7},{9,10},{10,9},{11,... | collective-permute-start | bytes 294920 | tf_op jit(solution)/shard_map/ppermute | solution.py:41
  21.5 5.8 %collective-permute-start.5 = (f32[3,32,128]{2,1,0:T(8,128)S(1)}, f32[3,32,128]{2,1,0:T(8,128)S(1)}, u32[]{:S(2)}, u32[]{:S(2)}) collective-permute-start(f32[3,32,128]{2,1,0:T(8,128)S(1)} %get-tuple-element.85), channel_id=1, source_target_pairs={{0,1},{1,0},{2,3},{3,2},{4,5},{5,4},{6,7},{7,6},{8,9},{9,8},{10,11... | collective-permute-start | bytes 147464 | tf_op jit(solution)/shard_map/ppermute | solution.py:41
  21.6 5.7 %collective-permute-start.6 = (f32[3,32,128]{2,1,0:T(8,128)S(1)}, f32[3,32,128]{2,1,0:T(8,128)S(1)}, u32[]{:S(2)}, u32[]{:S(2)}) collective-permute-start(f32[3,32,128]{2,1,0:T(8,128)S(1)} %get-tuple-element.86), channel_id=1, source_target_pairs={{1,2},{2,1},{3,4},{4,3},{5,6},{6,5},{7,0},{0,7},{9,10},{10,9},{11,... | collective-permute-start | bytes 147464 | tf_op jit(solution)/shard_map/ppermute | solution.py:41
  30.7 8.1 %collective-permute-start.7 = (f32[3,32,128]{2,1,0:T(8,128)S(1)}, f32[3,32,128]{2,1,0:T(8,128)S(1)}, u32[]{:S(2)}, u32[]{:S(2)}) collective-permute-start(f32[3,32,128]{2,1,0:T(8,128)S(1)} %get-tuple-element.94), channel_id=1, source_target_pairs={{0,1},{1,0},{2,3},{3,2},{4,5},{5,4},{6,7},{7,6},{8,9},{9,8},{10,11... | collective-permute-start | bytes 147464 | tf_op jit(solution)/shard_map/ppermute | solution.py:41
  31.6 7.2 %collective-permute-start.8 = (f32[3,32,128]{2,1,0:T(8,128)S(1)}, f32[3,32,128]{2,1,0:T(8,128)S(1)}, u32[]{:S(2)}, u32[]{:S(2)}) collective-permute-start(f32[3,32,128]{2,1,0:T(8,128)S(1)} %get-tuple-element.95), channel_id=1, source_target_pairs={{1,2},{2,1},{3,4},{4,3},{5,6},{6,5},{7,0},{0,7},{9,10},{10,9},{11,... | collective-permute-start | bytes 147464 | tf_op jit(solution)/shard_map/ppermute | solution.py:41
  34.1 4.8 %copy-start.6 = (f32[32]{0:T(128)S(1)}, f32[32]{0:T(128)}, u32[]{:S(2)}) copy-start(f32[32]{0:T(128)} %rest_0_.5) | copy-start | bytes 388
  42.2 2.9 %collective-permute-start.2 = (f32[6,64,128]{2,1,0:T(8,128)S(1)}, f32[6,64,128]{2,1,0:T(8,128)S(1)}, u32[]{:S(2)}, u32[]{:S(2)}) collective-permute-start(f32[6,64,128]{2,1,0:T(8,128)S(1)} %get-tuple-element.113), channel_id=1, source_target_pairs={{0,8},{8,0},{16,24},{24,16},{32,40},{40,32},{48,56},{56,48},{64,72... | collective-permute-start | bytes 589832 | tf_op jit(solution)/shard_map/cond/branch_0_fun/ppermute | solution.py:41
where the time goes:
time: 46.1 us; the launch traced here: 45.9 us
  Pallas kernels  29 us (63%)
  starting transfers between devices  11.5 us (25%)
  between operations  2.88 us (6%)
  other arithmetic  1.37 us (3%)
  waiting for transfers between devices  1.09 us (2%)
    ppermute x7, starting transfers between devices, swapped(): return lax.ppermute(shard, axis, pairs)  11.5 us
    pallas_call x3, Pallas kernels, local(): edge_call(step == 0, last, kick)  11.1 us
    pallas_call x2, Pallas kernels, local(): local_call(False)  9.56 us
    pallas_call x1, Pallas kernels, local(): local_call(True)  6.45 us
    pallas_call x1, Pallas kernels, local(): pl.pallas_call(pack_kernel, out_shape=(sds((6, facing, CA), F32),) * 2, i...  1.87 us
    ppermute x7, waiting for transfers between devices, swapped(): return lax.ppermute(shard, axis, pairs)  1.09 us
  transfers between devices with their start and end apart: 7, of which 1 were waited for; matrix products, arithmetic and copies ran while one was open for 1% of the time, Pallas kernels for 35%

commit v1 on v0

--- a/solution.py
+++ b/solution.py
@@ -401,7 +401,13 @@
             props[c, pl.ds(k, 1), :] = raw[pl.ds(c, 1), pl.ds(k * CA, CA)]
 
 
-def pack_kernel(tops, bottoms, x_ref, raw, slots, tally, to_first, to_second, props):
+def pack_kernel(
+    tops, bottoms, mates, x_ref, raw, slots, tally, to_first, to_second, crossing, props
+):
+    across = jnp.int32(0)
+    for r in range(mates.shape[0]):
+        across = jnp.where((mates[r] != r) & (mates[r] != (r ^ 1)), 1, across)
+    crossing[0, 0] = across
     relay_properties(raw, props)
     width = slots.shape[1]
     for buffer in (to_first, to_second):
@@ -449,11 +455,11 @@
     sds = jax.ShapeDtypeStruct
     params = pltpu.CompilerParams(vmem_limit_bytes=VMEM_LIMIT)
 
-    to_first, to_second = pl.pallas_call(
+    to_first, to_second, crossing = pl.pallas_call(
         pack_kernel,
-        out_shape=(sds((6, facing, CA), F32),) * 2,
-        in_specs=[SMEM] * 2 + [VMEM] * 4,
-        out_specs=(VMEM,) * 2,
+        out_shape=(sds((6, facing, CA), F32),) * 2 + (sds((1, 1), jnp.int32),),
+        in_specs=[SMEM] * 3 + [VMEM] * 4,
+        out_specs=(VMEM, VMEM, SMEM),
         scratch_shapes=[pltpu.VMEM((2,) + shape[1:], F32)],
         compiler_params=pltpu.CompilerParams(vmem_limit_bytes=PACK_LIMIT),
         cost_estimate=pl.CostEstimate(
@@ -463,6 +469,7 @@
     )(
         top_edge_groups,
         bottom_edge_groups,
+        exchange_mate,
         x,
         atomic_properties,
         slots,
@@ -580,9 +587,6 @@
             second_x = swapped(to_second, "dom", 1, True)
 
     keep, near_mate, ratio = choice[0] > 0.5, choice[1] > 0.5, choice[2]
-    slot = jnp.arange(exchange_mate.shape[0], dtype=jnp.int32)
-    crossing = jnp.any((exchange_mate != slot) & (exchange_mate != (slot ^ 1)))
-
     def exchanged(state, *others):
         def part(k):
             own, *rest = [a[3 * k : 3 * k + 3] for a in (state, *others)]
@@ -597,7 +601,7 @@
     def without_crossing(state):
         return exchanged(state, swapped(state, "rep", 0))
 
-    new_x, new_v = lax.cond(crossing, with_crossing, without_crossing, state)
+    new_x, new_v = lax.cond(crossing[0, 0] > 0, with_crossing, without_crossing, state)
     return new_x.reshape(3, 1, atoms), new_v.reshape(3, 1, atoms)
 
 

time: 46.1 us -> 54.6 us (1.18)
  starting transfers between devices: 11.5 us -> 16.3 us
  waiting for transfers between devices: 1.09 us -> 5.35 us
  other arithmetic: 1.37 us -> 0.74 us
    ppermute x7 -> x8, starting transfers between devices: 11.5 us -> 16.3 us  [swapped(): return lax.ppermute(shard, axis, pairs)]
    ppermute x7 -> x8, waiting for transfers between devices: 1.09 us -> 5.35 us  [swapped(): return lax.ppermute(shard, axis, pairs)]
    reduce_or x1 -> x0, other arithmetic: 0.66 us -> none  [local(): crossing = jnp.any((exchange_mate != slot) & (exchange_mate != slot ^ 1))]
  transfers between devices with their start and end apart: 7 -> 8, of which waited for: 1 -> 1; matrix products, arithmetic and copies ran while one was open for 1% -> 0% of each run, Pallas kernels for 35% -> 29%
where the time goes in v1:
time: 54.6 us; the launch traced here: 54.4 us
  Pallas kernels  29 us (53%)
  starting transfers between devices  16.3 us (30%)
  waiting for transfers between devices  5.35 us (10%)
  between operations  2.92 us (5%)
  other arithmetic  0.74 us (1%)
    ppermute x8, starting transfers between devices, swapped(): return lax.ppermute(shard, axis, pairs)  16.3 us
    pallas_call x3, Pallas kernels, local(): edge_call(step == 0, last, kick)  11.1 us
    pallas_call x2, Pallas kernels, local(): local_call(False)  9.55 us
    pallas_call x1, Pallas kernels, local(): local_call(True)  6.45 us
    ppermute x8, waiting for transfers between devices, swapped(): return lax.ppermute(shard, axis, pairs)  5.35 us
    pallas_call x1, Pallas kernels, local(): pl.pallas_call(pack_kernel, out_shape=(sds((6, facing, CA), F32),) * 2 +...  1.9 us
  transfers between devices with their start and end apart: 8, of which 1 were waited for; matrix products, arithmetic and copies ran while one was open for 0% of the time, Pallas kernels for 29%

profile of v1, /device:TPU:1, one launch (start us, length us, event | category | flops | bytes accessed | tf_op | source)
XLA Modules:
  0.0 54.4 jit_solution(9390948092983558290)
XLA Ops:
  0.6 0.0 copy-start.7
  0.6 0.0 copy-start
  0.7 0.0 copy-start.9
  1.4 1.9 %pack.1 = (f32[6,32,128]{2,1,0:T(8,128)}, f32[6,32,128]{2,1,0:T(8,128)}, s32[1,1]{1,0:T(1,128)}) custom-call(s32[1,32]{1,0:T(1,128)} %tops.7, s32[1,32]{1,0:T(1,128)} %bottoms.7, s32[32]{0:T(128)} %rest_1_.1, f32[3,64,128]{2,1,0:T(8,128)} %bitcast.12, f32[3,8192]{1,0:T(4,128)} %props.1, s32[2,32]{1,0:T(2,128)} %bitcast.19, s32[1,1]{1,0:T(1,128)S(6)} %copy.23.tally.rest_0_.rest_2_), custom_call_target="tpu_custom_call" | custom-call | flops 2000000000 | bytes 1000000 | tf_op jit(solution)/shard_map/pack/pallas_call | solution.py:458
  3.3 0.0 copy-start.2
  3.3 0.0 copy-start.3
  3.3 0.0 copy-start.4
  3.3 0.0 copy-start.8
  3.3 2.1 %collective-permute-start.3 = (f32[6,32,128]{2,1,0:T(8,128)}, f32[6,32,128]{2,1,0:T(8,128)S(1)}, u32[]{:S(2)}, u32[]{:S(2)}) collective-permute-start(f32[6,32,128]{2,1,0:T(8,128)} %get-tuple-element.76), channel_id=1, source_target_pairs={{0,1},{1,0},{2,3},{3,2},{4,5},{5,4},{6,7},{7,6},{8,9},{9,8},{10,11... | collective-permute-start | bytes 294920 | tf_op jit(solution)/shard_map/ppermute | solution.py:41
  5.4 3.2 %collective-permute-start.4 = (f32[6,32,128]{2,1,0:T(8,128)}, f32[6,32,128]{2,1,0:T(8,128)S(1)}, u32[]{:S(2)}, u32[]{:S(2)}) collective-permute-start(f32[6,32,128]{2,1,0:T(8,128)} %get-tuple-element.77), channel_id=1, source_target_pairs={{1,2},{2,1},{3,4},{4,3},{5,6},{6,5},{7,0},{0,7},{9,10},{10,9},{11,... | collective-permute-start | bytes 294920 | tf_op jit(solution)/shard_map/ppermute | solution.py:41
  10.0 6.4 %resident.3 = (f32[512,128]{1,0:T(8,128)S(1)}, f32[3,64,128]{2,1,0:T(8,128)S(1)}, bf16[64,2,16,128]{3,2,1,0:T(8,128)(2,1)S(1)}, f32[64,128]{1,0:T(8,128)S(1)}, f...) custom-call(s32[2,64]{1,0:T(2,128)S(1)} %bitcast.16, ...), custom_call_target="tpu_custom_call" | custom-call | flops 2000000000 | bytes 1000000 | tf_op jit(solution)/shard_map/resident/pallas_call | solution.py:552
  16.4 0.0 collective-permute-done.3.rest_8_.rest_10_.rest_12_
  16.4 0.0 collective-permute-done.4.rest_9_.rest_11_.rest_13_
  16.5 4.4 %edges.3 = (f32[3,64,128]{2,1,0:T(8,128)S(1)}, f32[3,64,128]{2,1,0:T(8,128)S(1)}, f32[3,32,128]{2,1,0:T(8,128)S(1)}, f32[3,32,128]{2,1,0:T(8,128)S(1)}, f32[64,128,128]{2,1,0:T(8,128)S(1)}) custom-call(s32[1,32]{1,0:T(1,128)S(1)} %copy-done.3, s32[1,32]{1,0:T(1,128)S(1)} %copy-done.4, s32[2,32]{1,0:T(2,128)S(1)} %bitcast.20, ...), custom_call_target="tpu_custom_call" | custom-call | flops 1000000000 | bytes 1000000 | tf_op jit(solution)/shard_map/edges/pallas_call | solution.py:561
  20.9 0.1 collective-permute-start.5
  21.0 0.9 %collective-permute-start.6 = (f32[3,32,128]{2,1,0:T(8,128)S(1)}, f32[3,32,128]{2,1,0:T(8,128)S(1)}, u32[]{:S(2)}, u32[]{:S(2)}) collective-permute-start(f32[3,32,128]{2,1,0:T(8,128)S(1)} %get-tuple-element.88), channel_id=1, source_target_pairs={{1,2},{2,1},{3,4},{4,3},{5,6},{6,5},{7,0},{0,7},{9,10},{10,9},{11,... | collective-permute-start | bytes 147464 | tf_op jit(solution)/shard_map/ppermute | solution.py:41
  21.9 4.8 %resident.4 = (f32[512,128]{1,0:T(8,128)S(1)}, f32[3,64,128]{2,1,0:T(8,128)S(1)}, bf16[64,2,16,128]{3,2,1,0:T(8,128)(2,1)S(1)}, f32[64,128]{1,0:T(8,128)S(1)}) custom-call(s32[2,64]{1,0:T(2,128)S(1)} %bitcast.17, s32[1,1]{1,0:T(1,128)S(6)} %copy.22.tally, f32[3,64,128]{2,1,0:T(8,128)S(1)} %get-tuple-element.78.x_ref.rest_1_.rest_0_, ...), custom_call_target="tpu_custom_call" | custom-call | flops 2000000000 | bytes 1000000 | tf_op jit(solution)/shard_map/resident/pallas_call | solution.py:556
  26.7 0.0 collective-permute-done.5.rest_8_
  26.7 0.0 collective-permute-done.6.rest_9_
  26.7 3.4 %edges.4 = (f32[3,64,128]{2,1,0:T(8,128)S(1)}, f32[3,64,128]{2,1,0:T(8,128)S(1)}, f32[3,32,128]{2,1,0:T(8,128)S(1)}, f32[3,32,128]{2,1,0:T(8,128)S(1)}) custom-call(s32[1,32]{1,0:T(1,128)S(1)} %copy-done.3, s32[1,32]{1,0:T(1,128)S(1)} %copy-done.4, s32[2,32]{1,0:T(2,128)S(1)} %bitcast.21, s32[1,1]{1,0:T(1,128)S(6)} %copy.23.tally.rest_0_.rest_2_, ...), custom_call_target="tpu_custom_call" | custom-call | flops 1000000000 | bytes 1000000 | tf_op jit(solution)/shard_map/edges/pallas_call | solution.py:561
  30.1 0.9 %collective-permute-start.7 = (f32[3,32,128]{2,1,0:T(8,128)S(1)}, f32[3,32,128]{2,1,0:T(8,128)S(1)}, u32[]{:S(2)}, u32[]{:S(2)}) collective-permute-start(f32[3,32,128]{2,1,0:T(8,128)S(1)} %get-tuple-element.96), channel_id=1, source_target_pairs={{0,1},{1,0},{2,3},{3,2},{4,5},{5,4},{6,7},{7,6},{8,9},{9,8},{10,11... | collective-permute-start | bytes 147464 | tf_op jit(solution)/shard_map/ppermute | solution.py:41
  31.0 2.5 %collective-permute-start.8 = (f32[3,32,128]{2,1,0:T(8,128)S(1)}, f32[3,32,128]{2,1,0:T(8,128)S(1)}, u32[]{:S(2)}, u32[]{:S(2)}) collective-permute-start(f32[3,32,128]{2,1,0:T(8,128)S(1)} %get-tuple-element.97), channel_id=1, source_target_pairs={{1,2},{2,1},{3,4},{4,3},{5,6},{6,5},{7,0},{0,7},{9,10},{10,9},{11,... | collective-permute-start | bytes 147464 | tf_op jit(solution)/shard_map/ppermute | solution.py:41
  33.5 4.8 %resident.5 = (f32[512,128]{1,0:T(8,128)S(1)}, f32[3,64,128]{2,1,0:T(8,128)S(1)}, bf16[64,2,16,128]{3,2,1,0:T(8,128)(2,1)S(1)}, f32[64,128]{1,0:T(8,128)S(1)}) custom-call(s32[2,64]{1,0:T(2,128)S(1)} %bitcast.18, s32[1,1]{1,0:T(1,128)S(6)} %copy.22.tally, f32[3,64,128]{2,1,0:T(8,128)S(1)} %get-tuple-element.90.x_ref.rest_3_, ...), custom_call_target="tpu_custom_call" | custom-call | flops 2000000000 | bytes 1000000 | tf_op jit(solution)/shard_map/resident/pallas_call | solution.py:556
  38.3 0.0 collective-permute-done.7.rest_10_
  38.3 0.0 collective-permute-done.8.rest_11_
  38.3 3.3 %edges.5 = (f32[6,64,128]{2,1,0:T(8,128)S(1)}, f32[8,128]{1,0:T(8,128)S(1)}) custom-call(s32[1,32]{1,0:T(1,128)S(1)} %copy-done.3, s32[1,32]{1,0:T(1,128)S(1)} %copy-done.4, s32[2,32]{1,0:T(2,128)S(1)} %bitcast.22, f32[32]{0:T(128)S(1)} %copy-done.6, s32[32]{0:T(128)S(1)} %copy-done.5, s32[1,1]{1,0:T(1,128)S(6)} %copy.23.tally.rest_0_.rest_2_, ...), custom_call_target="tpu_custom_call" | custom-call | flops 1000000000 | bytes 1000000 | tf_op jit(solution)/shard_map/edges/pallas_call | solution.py:561
  41.6 12.1 %conditional.1 = (pred[3,64,128]{2,1,0:T(8,128)(4,1)S(1)}, pred[3,64,128]{2,1,0:T(8,128)(4,1)S(1)}, f32[3,64,128]{2,1,0:T(8,128)S(1)}, f32[6,64,128]{2,1,0:T(8,1...) conditional(s32[]{:T(128)} %bitcast.3, (pred[128]{0:T(512)(128)(4,1)S(1)}, f32[6,64,128]{2,1,0:T(8,128)S(1)}, ...), branch_computations={%region_0.1_spmd, %region_1.2_spmd} | conditional | flops 49280 | bytes 2212996 | solution.py:604
  41.6 6.6 %collective-permute-start.1 = (f32[6,64,128]{2,1,0:T(8,128)S(1)}, f32[6,64,128]{2,1,0:T(8,128)S(1)}, u32[]{:S(2)}, u32[]{:S(2)}) collective-permute-start(f32[6,64,128]{2,1,0:T(8,128)S(1)} %get-tuple-element.121), channel_id=1, source_target_pairs={{8,16},{16,8},{24,32},{32,24},{40,48},{48,40},{56,64},{64,56},{72,... | collective-permute-start | bytes 589832 | tf_op jit(solution)/shard_map/cond/branch_1_fun/ppermute | solution.py:41
  48.2 0.1 collective-permute-start
  48.3 5.3 %collective-permute-done.1 = f32[6,64,128]{2,1,0:T(8,128)S(1)} collective-permute-done((f32[6,64,128]{2,1,0:T(8,128)S(1)}, f32[6,64,128]{2,1,0:T(8,128)S(1)}, u32[]{:S(2)}, u32[]{:S(2)}) %collective-permute-start.1) | collective-permute-done | bytes 196640 | tf_op jit(solution)/shard_map/cond/branch_1_fun/ppermute | solution.py:41
  53.7 0.0 collective-permute-done
  53.7 0.7 %select_multiply_fusion = (f32[3,64,128]{2,1,0:T(8,128)}, f32[3,64,128]{2,1,0:T(8,128)}) fusion(pred[3,64,128]{2,1,0:T(8,128)(4,1)S(1)} %get-tuple-element.100, f32[3,64,128]{2,1,0:T(8,128)S(1)} %get-tuple-element.103, f32[6,64,128]{2,1,0:T(8,128)S(1)} %get-tuple-element.101, f32[128]{0:T(128)S(1)} %bitcast.26, f32[3,64,128]{2,1,0:T(8,128)S(1)} %get-tuple-element.102), kind=kLoop, calls=%fused_computation.3 | loop fusion | flops 73728 | bytes 614912 | tf_op jit(solution)/shard_map/cond/branch_0_fun/mul | solution.py:596
  (19 shorter events, 0.1 us)
Async XLA Ops:
  0.6 9.3 %copy-start.7 = (f32[3,8192]{1,0:T(4,128)S(1)}, f32[3,8192]{1,0:T(4,128)}, u32[]{:S(2)}) copy-start(f32[3,8192]{1,0:T(4,128)} %props.1) | copy-start | bytes 294916
  0.6 9.3 %copy-start = (f32[3,1,8192]{2,1,0:T(1,128)S(1)}, f32[3,1,8192]{2,1,0:T(1,128)}, u32[]{:S(2)}) copy-start(f32[3,1,8192]{2,1,0:T(1,128)} %param.14) | copy-start | bytes 294916
  0.7 9.3 %copy-start.9 = (s32[2,4096]{1,0:T(2,128)S(1)}, s32[2,4096]{1,0:T(2,128)}, u32[]{:S(2)}) copy-start(s32[2,4096]{1,0:T(2,128)} %rest_0_.4) | copy-start | bytes 98308
  0.7 9.3 %copy-start.1 = (s32[2,1,64]{2,1,0:T(1,128)S(1)}, s32[2,1,64]{2,1,0:T(1,128)}, u32[]{:S(2)}) copy-start(s32[2,1,64]{2,1,0:T(1,128)} %param.17) | copy-start | bytes 1540
  3.3 13.2 %copy-start.2 = (s32[2,1,32]{2,1,0:T(1,128)S(1)}, s32[2,1,32]{2,1,0:T(1,128)}, u32[]{:S(2)}) copy-start(s32[2,1,32]{2,1,0:T(1,128)} %param.21) | copy-start | bytes 772
  3.3 13.2 %copy-start.3 = (s32[1,32]{1,0:T(1,128)S(1)}, s32[1,32]{1,0:T(1,128)}, u32[]{:S(2)}) copy-start(s32[1,32]{1,0:T(1,128)} %tops.7) | copy-start | bytes 388
  3.3 13.2 %copy-start.4 = (s32[1,32]{1,0:T(1,128)S(1)}, s32[1,32]{1,0:T(1,128)}, u32[]{:S(2)}) copy-start(s32[1,32]{1,0:T(1,128)} %bottoms.7) | copy-start | bytes 388
  3.3 13.2 %copy-start.8 = (f32[3,1,8192]{2,1,0:T(1,128)S(1)}, f32[3,1,8192]{2,1,0:T(1,128)}, u32[]{:S(2)}) copy-start(f32[3,1,8192]{2,1,0:T(1,128)} %param.15) | copy-start | bytes 294916
  3.3 13.1 %collective-permute-start.3 = (f32[6,32,128]{2,1,0:T(8,128)}, f32[6,32,128]{2,1,0:T(8,128)S(1)}, u32[]{:S(2)}, u32[]{:S(2)}) collective-permute-start(f32[6,32,128]{2,1,0:T(8,128)} %get-tuple-element.76), channel_id=1, source_target_pairs={{0,1},{1,0},{2,3},{3,2},{4,5},{5,4},{6,7},{7,6},{8,9},{9,8},{10,11... | collective-permute-start | bytes 294920 | tf_op jit(solution)/shard_map/ppermute | solution.py:41
  5.4 11.0 %collective-permute-start.4 = (f32[6,32,128]{2,1,0:T(8,128)}, f32[6,32,128]{2,1,0:T(8,128)S(1)}, u32[]{:S(2)}, u32[]{:S(2)}) collective-permute-start(f32[6,32,128]{2,1,0:T(8,128)} %get-tuple-element.77), channel_id=1, source_target_pairs={{1,2},{2,1},{3,4},{4,3},{5,6},{6,5},{7,0},{0,7},{9,10},{10,9},{11,... | collective-permute-start | bytes 294920 | tf_op jit(solution)/shard_map/ppermute | solution.py:41
  20.9 5.8 %collective-permute-start.5 = (f32[3,32,128]{2,1,0:T(8,128)S(1)}, f32[3,32,128]{2,1,0:T(8,128)S(1)}, u32[]{:S(2)}, u32[]{:S(2)}) collective-permute-start(f32[3,32,128]{2,1,0:T(8,128)S(1)} %get-tuple-element.87), channel_id=1, source_target_pairs={{0,1},{1,0},{2,3},{3,2},{4,5},{5,4},{6,7},{7,6},{8,9},{9,8},{10,11... | collective-permute-start | bytes 147464 | tf_op jit(solution)/shard_map/ppermute | solution.py:41
  21.0 5.7 %collective-permute-start.6 = (f32[3,32,128]{2,1,0:T(8,128)S(1)}, f32[3,32,128]{2,1,0:T(8,128)S(1)}, u32[]{:S(2)}, u32[]{:S(2)}) collective-permute-start(f32[3,32,128]{2,1,0:T(8,128)S(1)} %get-tuple-element.88), channel_id=1, source_target_pairs={{1,2},{2,1},{3,4},{4,3},{5,6},{6,5},{7,0},{0,7},{9,10},{10,9},{11,... | collective-permute-start | bytes 147464 | tf_op jit(solution)/shard_map/ppermute | solution.py:41
  30.1 8.1 %collective-permute-start.7 = (f32[3,32,128]{2,1,0:T(8,128)S(1)}, f32[3,32,128]{2,1,0:T(8,128)S(1)}, u32[]{:S(2)}, u32[]{:S(2)}) collective-permute-start(f32[3,32,128]{2,1,0:T(8,128)S(1)} %get-tuple-element.96), channel_id=1, source_target_pairs={{0,1},{1,0},{2,3},{3,2},{4,5},{5,4},{6,7},{7,6},{8,9},{9,8},{10,11... | collective-permute-start | bytes 147464 | tf_op jit(solution)/shard_map/ppermute | solution.py:41
  31.0 7.3 %collective-permute-start.8 = (f32[3,32,128]{2,1,0:T(8,128)S(1)}, f32[3,32,128]{2,1,0:T(8,128)S(1)}, u32[]{:S(2)}, u32[]{:S(2)}) collective-permute-start(f32[3,32,128]{2,1,0:T(8,128)S(1)} %get-tuple-element.97), channel_id=1, source_target_pairs={{1,2},{2,1},{3,4},{4,3},{5,6},{6,5},{7,0},{0,7},{9,10},{10,9},{11,... | collective-permute-start | bytes 147464 | tf_op jit(solution)/shard_map/ppermute | solution.py:41
  33.5 4.8 %copy-start.5 = (s32[32]{0:T(128)S(1)}, s32[32]{0:T(128)}, u32[]{:S(2)}) copy-start(s32[32]{0:T(128)} %rest_1_.1) | copy-start | bytes 388
  33.5 4.8 %copy-start.6 = (f32[32]{0:T(128)S(1)}, f32[32]{0:T(128)}, u32[]{:S(2)}) copy-start(f32[32]{0:T(128)} %rest_0_.5) | copy-start | bytes 388
  41.6 12.0 %collective-permute-start.1 = (f32[6,64,128]{2,1,0:T(8,128)S(1)}, f32[6,64,128]{2,1,0:T(8,128)S(1)}, u32[]{:S(2)}, u32[]{:S(2)}) collective-permute-start(f32[6,64,128]{2,1,0:T(8,128)S(1)} %get-tuple-element.121), channel_id=1, source_target_pairs={{8,16},{16,8},{24,32},{32,24},{40,48},{48,40},{56,64},{64,56},{72,... | collective-permute-start | bytes 589832 | tf_op jit(solution)/shard_map/cond/branch_1_fun/ppermute | solution.py:41
  48.2 5.4 %collective-permute-start = (f32[6,64,128]{2,1,0:T(8,128)S(1)}, f32[6,64,128]{2,1,0:T(8,128)S(1)}, u32[]{:S(2)}, u32[]{:S(2)}) collective-permute-start(f32[6,64,128]{2,1,0:T(8,128)S(1)} %get-tuple-element.121), channel_id=1, source_target_pairs={{0,8},{8,0},{16,24},{24,16},{32,40},{40,32},{48,56},{56,48},{64,72... | collective-permute-start | bytes 589832 | tf_op jit(solution)/shard_map/cond/branch_1_fun/ppermute | solution.py:41
